TPU v7x, 1024 devices: a whole 4x8x16 slice. The times are simulated.
1024 devices in a mesh: dp: 64 (over x, z_hi, y), tensor: 16 (over z_lo, core).
Axes of the slice: x: 4, y: 8, z: 16 (z_hi: 2, z_lo: 8; z = z_hi * 8 + z_lo), core: 2. Of those that a mesh axis runs over, the one named last changes fastest.
Arguments:
- activations: bfloat16 [8192, 8192], P('dp', 'tensor'), may hold values from -6 to 6
- projection: bfloat16 [8192, 128], replicated, may hold values from -0.5 to 0.5
- grad_gate: bfloat16 [8192, 28672], P('dp', 'tensor'), may hold values from -0.0078125 to 0.0078125
- grad_up: bfloat16 [8192, 28672], P('dp', 'tensor'), may hold values from -0.0078125 to 0.0078125
- first_moment: float32 [128, 2, 28672], P('dp', None, 'tensor'), may hold values from -0.625 to 0.625
- second_moment: float32 [128, 2, 28672], P('dp', None, 'tensor'), may hold values from 0.05 to 0.5
Outputs:
- gate_update: bfloat16 [8192, 28672], P('dp', 'tensor')
- up_update: bfloat16 [8192, 28672], P('dp', 'tensor')
- new_first: float32 [128, 2, 28672], P('dp', None, 'tensor')
- new_second: float32 [128, 2, 28672], P('dp', None, 'tensor')
All inputs are finite; a program needn't handle non-finite values.
Results may differ from a plain program's by a relative error of at most 0.015.
Values may be sent and summed in bfloat16 or wider, within the bound.
A program may use at most 32 MiB of HBM per device.

v0:
```python
import jax
import jax.numpy as jnp
from jax import lax
from jax.sharding import PartitionSpec as P

STEP = 1000


def shards(activations, projection, grad_gate, grad_up, first_moment, second_moment):
    feat_cols = activations.shape[1]
    ff_cols = grad_gate.shape[1]
    own_rows = first_moment.shape[0]
    proj_part = lax.dynamic_slice_in_dim(
        projection, lax.axis_index("tensor") * feat_cols, feat_cols, 0
    )
    partial_basis = jnp.dot(activations, proj_part, preferred_element_type=jnp.float32)
    token_basis = lax.psum(partial_basis.astype(jnp.bfloat16), "tensor")
    gate_part = jnp.einsum("tr,tc->rc", token_basis, grad_gate, preferred_element_type=jnp.float32)
    up_part = jnp.einsum("tr,tc->rc", token_basis, grad_up, preferred_element_type=jnp.float32)
    summed = lax.psum(jnp.stack([gate_part, up_part], axis=1), "dp")
    owned_grad = lax.dynamic_slice_in_dim(summed, lax.axis_index("dp") * own_rows, own_rows, 0)
    new_first = 0.9 * first_moment + 0.1 * owned_grad
    new_second = 0.999 * second_moment + 0.001 * owned_grad * owned_grad
    corr_one = 1.0 - 0.9**STEP
    corr_two = 1.0 - 0.999**STEP
    adam_step = new_first / corr_one / (jnp.sqrt(new_second / corr_two) + 1e-08)
    flat_step = adam_step.reshape(own_rows, 2 * ff_cols)
    out_rows = projection.shape[0] // lax.axis_size("dp")
    rows_proj = lax.dynamic_slice_in_dim(
        projection, lax.axis_index("dp") * out_rows, out_rows, 0
    ).astype(jnp.float32)
    gathered = lax.all_gather(flat_step, "dp", axis=0, tiled=True)
    update = jnp.dot(rows_proj, gathered, precision=lax.Precision.HIGHEST)
    gate_update = update[:, :ff_cols].astype(jnp.bfloat16)
    up_update = update[:, ff_cols:].astype(jnp.bfloat16)
    return (gate_update, up_update, new_first, new_second)


def solution(mesh):
    in_specs = (
        P("dp", "tensor"),
        P(),
        P("dp", "tensor"),
        P("dp", "tensor"),
        P("dp", None, "tensor"),
        P("dp", None, "tensor"),
    )
    out_specs = (
        P("dp", "tensor"),
        P("dp", "tensor"),
        P("dp", None, "tensor"),
        P("dp", None, "tensor"),
    )
    return jax.shard_map(shards, mesh=mesh, in_specs=in_specs, out_specs=out_specs, check_vma=False)
```

profile of v0, /device:TPU:1, one launch (start us, length us, event | category | flops | bytes accessed | tf_op | source)
XLA Modules:
  0.0 1433.3 jit_solution(5952274980121190713)
XLA Ops:
  7.2 0.0 copy-start
  7.2 0.0 copy-start.1
  7.2 0.0 all-reduce.2.cloned.1.call-start
  7.2 1.5 copy-done
  8.8 1.1 fusion
  9.9 95.2 %psum.14 = bf16[128,128]{0,1:T(8,128)(2,1)S(1)} all-reduce(bf16[128,128]{0,1:T(8,128)(2,1)S(1)} %fusion), channel_id=1, replica_groups=mesh['dp'=64,'tensor'=16] {'tensor'}, use_global_device_ids=true, to_apply=%region_0.0 | all-reduce | flops 16384 | bytes 65536 | tf_op jit(solution)/shard_map/psum | solution.py:17
  105.1 1.3 convolution_bitcast_fusion
  106.4 0.0 copy-done.1
  106.4 0.3 convolution_bitcast_fusion.1
  106.7 1.4 pad_maximum_fusion
  108.1 0.0 copy-start.2
  108.1 0.0 copy-start.3
  108.1 0.0 all-reduce.2.cloned.1.call-update
  108.1 0.0 all-gather.3.cloned.1.call-start
  108.1 1097.9 %all-reduce.2.cloned.1.call-done = f32[128,2,1792]{2,0,1:T(8,128)} async-done(((f32[128,2,1792]{2,0,1:T(8,128)}), f32[128,2,1792]{2,0,1:T(8,128)}) %all-reduce.2.cloned.1.call-update) | async-done | bytes 1835024 | tf_op jit(solution)/shard_map/psum | solution.py:20
  1206.1 0.0 copy-done.2
  1206.1 0.0 copy-done.3
  1206.1 1.6 add_divide_fusion
  1207.7 0.0 all-gather.3.cloned.1.call-update
  1207.7 0.6 copy.17
  1208.3 0.6 copy.16
  1209.0 210.6 %all-gather.3.cloned.1.call-done = f32[64,2,3584]{2,1,0:T(2,128)} async-done(((f32[1,2,3584]{2,1,0:T(2,128)}), f32[64,2,3584]{2,1,0:T(2,128)}) %all-gather.3.cloned.1.call-update) | async-done | bytes 1835024 | tf_op jit(solution)/shard_map/all_gather | solution.py:32
  1419.5 3.4 reshape.13
  1423.0 2.5 convolution_convert_fusion
  1425.5 1.0 fusion.9
Async XLA Ops:
  7.2 1.6 copy-start
  7.2 99.2 %copy-start.1 = (bf16[128,1792]{1,0:T(8,128)(2,1)S(1)}, bf16[128,1792]{1,0:T(8,128)(2,1)}, u32[]{:S(2)}) copy-start(bf16[128,1792]{1,0:T(8,128)(2,1)} %param.8) | copy-start | bytes 1376260
  7.2 1198.9 %all-reduce.2.cloned.1.call-start = ((), (), s32[]{:S(2)}) async-start(), calls=%async_computation | async-start | bytes 3670016 | tf_op jit(solution)/shard_map/psum | solution.py:20
  108.1 1098.0 %copy-start.2 = (f32[2,2,1792]{2,1,0:T(2,128)S(1)}, f32[2,2,1792]{2,1,0:T(2,128)}, u32[]{:S(2)}) copy-start(f32[2,2,1792]{2,1,0:T(2,128)} %param.11) | copy-start | bytes 86020
  108.1 1098.0 %copy-start.3 = (f32[2,2,1792]{2,1,0:T(2,128)S(1)}, f32[2,2,1792]{2,1,0:T(2,128)}, u32[]{:S(2)}) copy-start(f32[2,2,1792]{2,1,0:T(2,128)} %param.10) | copy-start | bytes 86020
  108.1 1311.4 %all-gather.3.cloned.1.call-start = ((), (), s32[]{:S(2)}) async-start(), calls=%async_computation.1 | async-start | bytes 1863680 | tf_op jit(solution)/shard_map/all_gather | solution.py:32
Sparse Core Ops, SparseCore 0:
  108.2 1097.8 all-reduce.1
  1212.4 207.0 all-gather.2
where the time goes:
time: 1440 us; the launch traced here: 1430 us
  waiting for transfers between devices  1310 us (91%)
  blocking collectives  95.2 us (7%)
    psum x1, waiting for transfers between devices, shards(): summed = lax.psum(jnp.stack([gate_part, up_part], axis=1), 'dp')  1100 us
    all_gather x1, waiting for transfers between devices, shards(): gathered = lax.all_gather(flat_step, 'dp', axis=0, tiled=True)  211 us
    psum x1, blocking collectives, shards(): token_basis = lax.psum(partial_basis.astype(jnp.bfloat16), 'tensor')  95.2 us
  transfers between devices with their start and end apart: 2, of which 2 were waited for; matrix products, arithmetic and copies ran while one was open for 0% of the time, Pallas kernels for 0%

commit v1 on v0

v1 whole, which is shorter than its diff:
```python
import dataclasses
import functools

import jax
import jax.numpy as jnp
from jax import lax
from jax.experimental import pallas as pl
from jax.experimental.pallas import tpu as pltpu
from jax.sharding import PartitionSpec as P

STEP = 1000
BF16 = jnp.bfloat16
F32 = jnp.float32
MESH = pl.DeviceIdType.MESH


@dataclasses.dataclass(frozen=True)
class Cfg:
    ny: int
    nzl: int
    tok: int
    feat: int
    ff: int
    chunks: tuple
    nx: int = 4

    @property
    def pieces(self):
        return self.nx * self.ny

    @property
    def rank(self):
        return 4 * self.pieces

    @property
    def half(self):
        return self.ff // 2

    @property
    def lanes(self):
        out, start = [], 0
        for width in self.chunks:
            out.append((start, width))
            start += width
        return out


def row_select(cfg):
    shape = (cfg.pieces, 16, cfg.rank)
    piece = lax.broadcasted_iota(jnp.int32, shape, 0)
    sub = lax.broadcasted_iota(jnp.int32, shape, 1)
    row = lax.broadcasted_iota(jnp.int32, shape, 2)
    ybits = cfg.ny.bit_length() - 1
    px = lax.shift_right_logical(piece, ybits)
    py = piece & (cfg.ny - 1)
    zh = lax.shift_right_logical(sub, 1) & 1
    target = (px * 2 + zh) * (2 * cfg.ny) + py * 2 + (sub & 1)
    return jnp.where(row == target, 1.0, 0.0).astype(BF16).reshape(cfg.pieces * 16, cfg.rank)


def dot(a, b):
    return jnp.dot(a, b, preferred_element_type=F32)


def dot_nt(a, b):
    return lax.dot_general(a, b, (((1,), (1,)), ((), ())), preferred_element_type=F32)


def comm_kernel(cfg, *refs):
    nk = len(cfg.chunks)
    nx, ny, nzl, half = cfg.nx, cfg.ny, cfg.nzl, cfg.half
    nyh, htok, wide = ny // 2, cfg.tok // 2, cfg.pieces * 16
    (act, proj, gg, gu, m1, m2), refs = refs[:6], refs[6:]
    g_outs, refs = refs[:nk], refs[nk:]
    (pw_out, nf_out, ns_out), refs = refs[:3], refs[3:]
    (act_v, pp_v, g_v, pr_v, sel_v, pw_v, w_v, mm, ml, nfl, nsl), refs = refs[:11], refs[11:]
    (part_v, csend, crecv, zsend, zrecv, basis_v), refs = refs[:6], refs[6:]
    names = ("p", "rx1", "sx2", "rx2", "sy", "ry", "sz", "rz", "tf", "g")
    bufs = {}
    for name in names:
        bufs[name], refs = refs[:nk], refs[nk:]
    load_sem, send_sem, recv_sem = refs

    dp, tensor = lax.axis_index("dp"), lax.axis_index("tensor")
    core, zl = tensor % 2, tensor // 2
    y, zh, x = dp % ny, (dp // ny) % 2, dp // (2 * ny)
    xa = x + 1 - 2 * (x % 2)
    xb = (nx - 1) - x
    xo = (x + 2) % nx

    def at_x(other):
        return ((other * 2 + zh) * ny + y, tensor)

    def at_y(d):
        return ((x * 2 + zh) * ny + (y + d) % ny, tensor)

    def at_z(d):
        return (dp, ((zl + d) % nzl) * 2 + core)

    core_peer = (dp, zl * 2 + 1 - core)
    far_peer = ((x * 2 + 1 - zh) * ny + y, tensor)
    partners = [core_peer, far_peer, at_x(xa), at_x(xb)]
    partners += [at_z(d) for d in range(1, nzl)] + [at_y(d) for d in range(1, ny)]

    counts = {"local": 0, "remote": 0}
    remote = []

    def local_copy(src, dst):
        copy = pltpu.make_async_copy(src, dst, load_sem.at[counts["local"]])
        counts["local"] += 1
        copy.start()
        return copy

    def send(src, dst, device):
        index = counts["remote"]
        counts["remote"] += 1
        copy = pltpu.make_async_remote_copy(
            src_ref=src,
            dst_ref=dst,
            send_sem=send_sem.at[index],
            recv_sem=recv_sem.at[index],
            device_id=device,
            device_id_type=MESH,
        )
        copy.start()
        remote.append(copy)
        return copy

    load_act = local_copy(act, act_v)
    load_pp = local_copy(proj.at[pl.ds(pl.multiple_of(tensor * cfg.feat, cfg.feat), cfg.feat)], pp_v)
    barrier = pltpu.get_barrier_semaphore()
    for partner in partners:
        pl.semaphore_signal(barrier, inc=1, device_id=partner, device_id_type=MESH)
    out_rows = pr_v.shape[0]
    load_pr = local_copy(proj.at[pl.ds(pl.multiple_of(dp * out_rows, out_rows), out_rows)], pr_v)
    load_m = [local_copy(m1, mm.at[zh, 0]), local_copy(m2, mm.at[zh, 1])]
    load_g = []
    for q, (ref, h) in enumerate(((gg, 0), (gg, 1), (gu, 0), (gu, 1))):
        load_g.append(local_copy(ref.at[:, pl.ds(h * half, half)], g_v.at[pl.ds(q * cfg.tok, cfg.tok)]))

    load_act.wait()
    load_pp.wait()
    part = dot(act_v[...], pp_v[...])
    part_v[...] = part.reshape(2, htok, cfg.rank)
    csend[...] = part_v[1 - core].astype(BF16)
    sel_v[...] = row_select(cfg)
    for copy in load_m:
        copy.wait()

    pl.semaphore_wait(barrier, len(partners))

    to_core = send(csend, crecv, core_peer)
    moments = send(mm.at[zh], mm.at[zh], far_peer)
    load_pr.wait()
    rows_wide = dot_nt(pr_v[...], sel_v[...])
    lane_quarter = lax.shift_right_logical(lax.broadcasted_iota(jnp.int32, rows_wide.shape, 1), 2) & 3
    for q in range(4):
        pw_v[q] = jnp.where(lane_quarter == q, rows_wide, 0.0).astype(BF16)
    save_pw = local_copy(pw_v, pw_out)
    to_core.wait_recv()
    mine = part_v[core] + crecv[...].astype(F32)
    zsend[...] = mine.astype(BF16)
    part_v[core] = mine
    to_chips = [send(zsend, zrecv.at[d - 1], at_z(d)) for d in range(1, nzl)]
    for copy in load_g:
        copy.wait()
    for copy in to_chips:
        copy.wait_recv()
    total = part_v[core]
    for d in range(1, nzl):
        total = total + zrecv[d - 1].astype(F32)
    basis_v[core] = total.astype(BF16)
    finished = send(basis_v.at[core], basis_v.at[core], core_peer)
    finished.wait_recv()

    basis = basis_v[...].reshape(cfg.tok, cfg.rank)
    basis_wide = dot_nt(sel_v[...], basis)
    sub_quarter = lax.shift_right_logical(lax.broadcasted_iota(jnp.int32, basis_wide.shape, 0), 2) & 3
    for q in range(4):
        w_v[:, q * cfg.tok : (q + 1) * cfg.tok] = jnp.where(sub_quarter == q, basis_wide, 0.0).astype(BF16)

    def block(xblock, colour):
        return pl.ds(xblock * ny + colour * nyh, nyh)

    first = []
    for k, (start, width) in enumerate(cfg.lanes):
        p, rx1 = bufs["p"][k], bufs["rx1"][k]
        grads = g_v[:, start : start + width]
        p[...] = dot(w_v[...], grads).astype(BF16).reshape(cfg.pieces, 16, width)
        first.append(
            [
                send(p.at[block(xa, 0)], rx1.at[0, 0], at_x(xa)),
                send(p.at[block(xb, 1)], rx1.at[1, 0], at_x(xb)),
                send(p.at[block(xo, 0)], rx1.at[0, 1], at_x(xa)),
                send(p.at[block(xo, 1)], rx1.at[1, 1], at_x(xb)),
            ]
        )

    moments.wait_recv()
    for which in range(2):
        for end in range(2):
            for j in range(2):
                for q in range(4):
                    ml[which, pl.ds(4 * q + 2 * end + j, 1), :] = mm[
                        end, which, j, pl.ds(q // 2, 1), pl.ds((q % 2) * half, half)
                    ]

    second = []
    for k in range(nk):
        p, rx1, sx2, rx2 = (bufs[name][k] for name in ("p", "rx1", "sx2", "rx2"))
        for copy in first[k]:
            copy.wait_recv()
        copies = []
        for colour, other in ((0, xb), (1, xa)):
            sx2[colour] = (p[block(other, colour)].astype(F32) + rx1[colour, 1].astype(F32)).astype(BF16)
            copies.append(send(sx2.at[colour], rx2.at[colour], at_x(other)))
        second.append(copies)

    third = []
    for k in range(nk):
        p, rx1, rx2, sy, ry = (bufs[name][k] for name in ("p", "rx1", "rx2", "sy", "ry"))
        for copy in second[k]:
            copy.wait_recv()
        for colour in range(2):
            own = p[block(x, colour)].astype(F32) + rx1[colour, 0].astype(F32) + rx2[colour].astype(F32)
            sy[pl.ds(colour * nyh, nyh)] = own.astype(BF16)
        third.append([send(sy.at[(y + d) % ny], ry.at[d - 1], at_y(d)) for d in range(1, ny)])

    fourth = []
    for k in range(nk):
        sy, ry, sz, rz, tf = (bufs[name][k] for name in ("sy", "ry", "sz", "rz", "tf"))
        for copy in third[k]:
            copy.wait_recv()
        total = sy[y].astype(F32)
        for d in range(1, ny):
            total = total + ry[d - 1].astype(F32)
        tf[...] = total
        sz[...] = total.astype(BF16)
        fourth.append(send(sz, rz, far_peer))

    corr_one = 1.0 - 0.9**STEP
    corr_two = 1.0 - 0.999**STEP
    fifth = []
    for k, (start, width) in enumerate(cfg.lanes):
        rz, tf, g = (bufs[name][k] for name in ("rz", "tf", "g"))
        fourth[k].wait_recv()
        cols = pl.ds(start, width)
        grad = tf[...] + rz[...].astype(F32)
        new_first = 0.9 * ml[0, :, cols] + 0.1 * grad
        new_second = 0.999 * ml[1, :, cols] + 0.001 * grad * grad
        step = new_first / corr_one / (jnp.sqrt(new_second / corr_two) + 1e-08)
        g[x * ny + y] = step.astype(BF16)
        fifth.append([send(g.at[x * ny + y], g.at[x * ny + y], at_y(d)) for d in range(1, ny)])
        nfl[:, cols] = new_first
        nsl[:, cols] = new_second

    sixth = []
    for k in range(nk):
        g = bufs["g"][k]
        for copy in fifth[k]:
            copy.wait_recv()
        copies = []
        for colour, near, far in ((0, xb, xa), (1, xa, xb)):
            copies.append(send(g.at[block(x, colour)], g.at[block(x, colour)], at_x(near)))
        for colour, near, far in ((0, xb, xa), (1, xa, xb)):
            copies.append(send(g.at[block(x, colour)], g.at[block(x, colour)], at_x(far)))
        sixth.append(copies)

    for j in range(2):
        for q in range(4):
            for flat, out in ((nfl, nf_out), (nsl, ns_out)):
                out[j, pl.ds(q // 2, 1), pl.ds((q % 2) * half, half)] = flat[pl.ds(4 * q + j + 2 * zh, 1), :]

    seventh = []
    for k in range(nk):
        g = bufs["g"][k]
        copies = []
        for colour, near, far in ((0, xb, xa), (1, xa, xb)):
            sixth[k][colour].wait_recv()
            copies.append(send(g.at[block(near, colour)], g.at[block(near, colour)], at_x(far)))
        seventh.append(copies)

    saves = []
    for k in range(nk):
        for copy in sixth[k][2:] + seventh[k]:
            copy.wait_recv()
        saves.append(local_copy(bufs["g"][k], g_outs[k]))
    for copy in remote:
        copy.wait_send()
    save_pw.wait()
    for copy in saves:
        copy.wait()


def update_kernel(cfg, *refs):
    nk = len(cfg.chunks)
    gs, refs = refs[:nk], refs[nk:]
    pw, nf, ns, gate, up, nf_out, ns_out, refs = *refs[:7], refs[7:]
    g_vs, refs = refs[:nk], refs[nk:]
    out_vs, refs = refs[:nk], refs[nk:]
    pw_v, sem = refs
    loads = [pltpu.make_async_copy(pw, pw_v, sem.at[0])]
    loads += [pltpu.make_async_copy(gs[k], g_vs[k], sem.at[1 + k]) for k in range(nk)]
    for copy in loads:
        copy.start()
    nf_out[...] = nf[...]
    ns_out[...] = ns[...]
    loads[0].wait()
    saves = []
    for k, (start, width) in enumerate(cfg.lanes):
        loads[1 + k].wait()
        steps = g_vs[k][...].reshape(cfg.pieces * 16, width)
        for q, out in enumerate((gate, gate, up, up)):
            out_vs[k][q] = dot(pw_v[q], steps).astype(BF16)
            columns = pl.ds((q % 2) * cfg.half + start, width)
            copy = pltpu.make_async_copy(out_vs[k].at[q], out.at[:, columns], sem.at[1 + nk + 4 * k + q])
            copy.start()
            saves.append(copy)
    for copy in saves:
        copy.wait()


def shards(cfg, activations, projection, grad_gate, grad_up, first_moment, second_moment):
    nk = len(cfg.chunks)
    out_rows = projection.shape[0] // (2 * cfg.pieces)
    wide, nyh, htok = cfg.pieces * 16, cfg.ny // 2, cfg.tok // 2
    any_spec = pl.BlockSpec(memory_space=pl.ANY)
    vmem_spec = pl.BlockSpec(memory_space=pltpu.VMEM)
    small = jax.ShapeDtypeStruct(first_moment.shape, F32)

    def chunked(*shape, dtype=BF16):
        return [pltpu.VMEM((*shape, width), dtype) for width in cfg.chunks]

    remote_copies = 3 + (cfg.nzl - 1) + nk * (4 + 2 + 2 * (cfg.ny - 1) + 1 + 6)
    scratch = [
        pltpu.VMEM((cfg.tok, cfg.feat), BF16),
        pltpu.VMEM((cfg.feat, cfg.rank), BF16),
        pltpu.VMEM((4 * cfg.tok, cfg.half), BF16),
        pltpu.VMEM((out_rows, cfg.rank), BF16),
        pltpu.VMEM((wide, cfg.rank), BF16),
        pltpu.VMEM((4, out_rows, wide), BF16),
        pltpu.VMEM((wide, 4 * cfg.tok), BF16),
        pltpu.VMEM((2, 2, 2, 2, cfg.ff), F32),
        pltpu.VMEM((2, 16, cfg.half), F32),
        pltpu.VMEM((16, cfg.half), F32),
        pltpu.VMEM((16, cfg.half), F32),
        pltpu.VMEM((2, htok, cfg.rank), F32),
        pltpu.VMEM((htok, cfg.rank), BF16),
        pltpu.VMEM((htok, cfg.rank), BF16),
        pltpu.VMEM((htok, cfg.rank), BF16),
        pltpu.VMEM((cfg.nzl - 1, htok, cfg.rank), BF16),
        pltpu.VMEM((2, htok, cfg.rank), BF16),
        *chunked(cfg.pieces, 16),
        *chunked(2, 2, nyh, 16),
        *chunked(2, nyh, 16),
        *chunked(2, nyh, 16),
        *chunked(cfg.ny, 16),
        *chunked(cfg.ny - 1, 16),
        *chunked(16),
        *chunked(16),
        *chunked(16, dtype=F32),
        *chunked(cfg.pieces, 16),
        pltpu.SemaphoreType.DMA((10 + nk,)),
        pltpu.SemaphoreType.DMA((remote_copies,)),
        pltpu.SemaphoreType.DMA((remote_copies,)),
    ]
    gathered = [jax.ShapeDtypeStruct((cfg.pieces, 16, width), BF16) for width in cfg.chunks]
    *steps, rows_wide, new_first, new_second = pl.pallas_call(
        functools.partial(comm_kernel, cfg),
        out_shape=(*gathered, jax.ShapeDtypeStruct((4, out_rows, wide), BF16), small, small),
        in_specs=[any_spec] * 6,
        out_specs=(*[any_spec] * nk, any_spec, vmem_spec, vmem_spec),
        scratch_shapes=scratch,
        compiler_params=pltpu.CompilerParams(collective_id=0, has_side_effects=True, vmem_limit_bytes=48 << 20),
        name="comm",
    )(activations, projection, grad_gate, grad_up, first_moment, second_moment)
    update = jax.ShapeDtypeStruct((out_rows, cfg.ff), BF16)
    return pl.pallas_call(
        functools.partial(update_kernel, cfg),
        out_shape=(update, update, small, small),
        in_specs=[any_spec] * (nk + 1) + [vmem_spec] * 2,
        out_specs=(any_spec, any_spec, vmem_spec, vmem_spec),
        scratch_shapes=[
            *chunked(cfg.pieces, 16),
            *chunked(4, out_rows),
            pltpu.VMEM((4, out_rows, wide), BF16),
            pltpu.SemaphoreType.DMA((1 + 5 * nk,)),
        ],
        compiler_params=pltpu.CompilerParams(vmem_limit_bytes=48 << 20),
        name="update",
    )(*steps, rows_wide, new_first, new_second)


def build(mesh, cfg):
    in_specs = (
        P("dp", "tensor"),
        P(),
        P("dp", "tensor"),
        P("dp", "tensor"),
        P("dp", None, "tensor"),
        P("dp", None, "tensor"),
    )
    out_specs = (
        P("dp", "tensor"),
        P("dp", "tensor"),
        P("dp", None, "tensor"),
        P("dp", None, "tensor"),
    )
    return jax.shard_map(
        functools.partial(shards, cfg), mesh=mesh, in_specs=in_specs, out_specs=out_specs, check_vma=False
    )


def solution(mesh):
    return build(mesh, Cfg(ny=8, nzl=8, tok=128, feat=512, ff=1792, chunks=(512, 384)))
```

time: 1440 us -> 84.9 us (0.06)
  the two profiles are of different devices: /device:TPU:1 before, /device:TPU:64 now
where the time goes in v1:
time: 84.9 us; the launch traced here: 84.5 us
  Pallas kernels  77.9 us (92%)
  local copies, waits for them, and re-layouts  6.02 us (7%)
    pallas_call x1, Pallas kernels, shards(): pl.pallas_call(functools.partial(comm_kernel, cfg), out_shape=(*gathered,...  75.4 us
    unnamed x12, local copies, waits for them, and re-layouts  6.02 us
    pallas_call x1, Pallas kernels, shards(): pl.pallas_call(functools.partial(update_kernel, cfg), out_shape=(update,...  2.51 us

profile of v1, /device:TPU:64, one launch (start us, length us, event | category | flops | bytes accessed | tf_op | source)
XLA Modules:
  0.0 84.5 jit_solution(7122336663991459704)
XLA Ops:
  0.6 0.0 copy-start
  0.6 1.6 %copy-done = bf16[8192,128]{1,0:T(8,128)(2,1)S(1)} copy-done((bf16[8192,128]{1,0:T(8,128)(2,1)S(1)}, bf16[8192,128]{1,0:T(8,128)(2,1)}, u32[]{:S(2)}) %copy-start) | copy-done | bytes 2097176
  2.2 0.0 copy-start.1
  2.2 1.0 %copy-done.1 = bf16[128,1792]{1,0:T(8,128)(2,1)S(1)} copy-done((bf16[128,1792]{1,0:T(8,128)(2,1)S(1)}, bf16[128,1792]{1,0:T(8,128)(2,1)}, u32[]{:S(2)}) %copy-start.1) | copy-done | bytes 458776
  3.2 0.0 copy-start.2
  3.2 1.0 %copy-done.2 = bf16[128,1792]{1,0:T(8,128)(2,1)S(1)} copy-done((bf16[128,1792]{1,0:T(8,128)(2,1)S(1)}, bf16[128,1792]{1,0:T(8,128)(2,1)}, u32[]{:S(2)}) %copy-start.2) | copy-done | bytes 458776
  4.3 0.0 copy-start.3
  4.3 0.9 %copy-done.3 = bf16[128,512]{1,0:T(8,128)(2,1)S(1)} copy-done((bf16[128,512]{1,0:T(8,128)(2,1)S(1)}, bf16[128,512]{1,0:T(8,128)(2,1)}, u32[]{:S(2)}) %copy-start.3) | copy-done | bytes 131096
  5.2 0.0 copy-start.4
  5.2 0.7 copy-done.4
  5.9 0.0 copy-start.5
  5.9 0.7 copy-done.5
  6.7 75.4 %comm.1 = (bf16[32,16,512]{2,1,0:T(8,128)(2,1)S(1)}, bf16[32,16,384]{2,1,0:T(8,128)(2,1)S(1)}, bf16[4,128,512]{2,1,0:T(8,128)(2,1)S(1)}, f32[2,2,1792]{2,1,0:T(2,128)S(1)}, f32[2,2,1792]{2,1,0:T(2,128)S(1)}) custom-call(bf16[128,512]{1,0:T(8,128)(2,1)S(1)} %copy-done.3, bf16[8192,128]{1,0:T(8,128)(2,1)S(1)} %copy-done, bf16[128,1792]{1,0:T(8,128)(2,1)S(1)} %copy-done.1, ...), custom_call_target="tpu_custom_call" | custom-call | tf_op jit(solution)/shard_map/comm/pallas_call | solution.py:368
  82.0 2.5 %update.1 = (bf16[128,1792]{1,0:T(8,128)(2,1)}, bf16[128,1792]{1,0:T(8,128)(2,1)}, f32[2,2,1792]{2,1,0:T(2,128)}, f32[2,2,1792]{2,1,0:T(2,128)}) custom-call(bf16[32,16,512]{2,1,0:T(8,128)(2,1)S(1)} %get-tuple-element.9.refs_0_, bf16[32,16,384]{2,1,0:T(8,128)(2,1)S(1)} %get-tuple-element.10.refs_1_, bf16[4,128,512]{2,1,0:T(8,128)(2,1)S(1)} %get-tuple-element.11.refs_2_, ...), custom_call_target="tpu_custom_call" | custom-call | tf_op jit(solution)/shard_map/update/pallas_call | solution.py:378
Async XLA Ops:
  0.6 1.6 %copy-start = (bf16[8192,128]{1,0:T(8,128)(2,1)S(1)}, bf16[8192,128]{1,0:T(8,128)(2,1)}, u32[]{:S(2)}) copy-start(bf16[8192,128]{1,0:T(8,128)(2,1)} %refs_1_.1) | copy-start | bytes 6291460
  2.2 1.0 %copy-start.1 = (bf16[128,1792]{1,0:T(8,128)(2,1)S(1)}, bf16[128,1792]{1,0:T(8,128)(2,1)}, u32[]{:S(2)}) copy-start(bf16[128,1792]{1,0:T(8,128)(2,1)} %refs_2_.1) | copy-start | bytes 1376260
  3.2 1.0 %copy-start.2 = (bf16[128,1792]{1,0:T(8,128)(2,1)S(1)}, bf16[128,1792]{1,0:T(8,128)(2,1)}, u32[]{:S(2)}) copy-start(bf16[128,1792]{1,0:T(8,128)(2,1)} %refs_3_.1) | copy-start | bytes 1376260
  4.3 0.9 %copy-start.3 = (bf16[128,512]{1,0:T(8,128)(2,1)S(1)}, bf16[128,512]{1,0:T(8,128)(2,1)}, u32[]{:S(2)}) copy-start(bf16[128,512]{1,0:T(8,128)(2,1)} %refs_0_.1) | copy-start | bytes 393220
  5.2 0.7 copy-start.4
  5.9 0.7 copy-start.5

commit v2 on v1

--- a/solution.py
+++ b/solution.py
@@ -37,16 +37,12 @@
         return self.ff // 2
 
     @property
-    def lanes(self):
-        out, start = [], 0
-        for width in self.chunks:
-            out.append((start, width))
-            start += width
-        return out
+    def widths(self):
+        return [width for _, _, width in self.chunks]
 
 
 def row_select(cfg):
-    shape = (cfg.pieces, 16, cfg.rank)
+    shape = (cfg.pieces, 8, cfg.rank)
     piece = lax.broadcasted_iota(jnp.int32, shape, 0)
     sub = lax.broadcasted_iota(jnp.int32, shape, 1)
     row = lax.broadcasted_iota(jnp.int32, shape, 2)
@@ -55,7 +51,7 @@
     py = piece & (cfg.ny - 1)
     zh = lax.shift_right_logical(sub, 1) & 1
     target = (px * 2 + zh) * (2 * cfg.ny) + py * 2 + (sub & 1)
-    return jnp.where(row == target, 1.0, 0.0).astype(BF16).reshape(cfg.pieces * 16, cfg.rank)
+    return jnp.where(row == target, 1.0, 0.0).astype(BF16).reshape(cfg.pieces * 8, cfg.rank)
 
 
 def dot(a, b):
@@ -69,7 +65,7 @@
 def comm_kernel(cfg, *refs):
     nk = len(cfg.chunks)
     nx, ny, nzl, half = cfg.nx, cfg.ny, cfg.nzl, cfg.half
-    nyh, htok, wide = ny // 2, cfg.tok // 2, cfg.pieces * 16
+    nyh, htok = ny // 2, cfg.tok // 2
     (act, proj, gg, gu, m1, m2), refs = refs[:6], refs[6:]
     g_outs, refs = refs[:nk], refs[nk:]
     (pw_out, nf_out, ns_out), refs = refs[:3], refs[3:]
@@ -97,6 +93,8 @@
     def at_z(d):
         return (dp, ((zl + d) % nzl) * 2 + core)
 
+    y_order = sorted(range(1, ny), key=lambda d: -min(d, ny - d))
+    z_order = list(range(nzl - 1, 0, -1))
     core_peer = (dp, zl * 2 + 1 - core)
     far_peer = ((x * 2 + 1 - zh) * ny + y, tensor)
     partners = [core_peer, far_peer, at_x(xa), at_x(xb)]
@@ -135,8 +133,11 @@
     load_pr = local_copy(proj.at[pl.ds(pl.multiple_of(dp * out_rows, out_rows), out_rows)], pr_v)
     load_m = [local_copy(m1, mm.at[zh, 0]), local_copy(m2, mm.at[zh, 1])]
     load_g = []
-    for q, (ref, h) in enumerate(((gg, 0), (gg, 1), (gu, 0), (gu, 1))):
-        load_g.append(local_copy(ref.at[:, pl.ds(h * half, half)], g_v.at[pl.ds(q * cfg.tok, cfg.tok)]))
+    for which, ref in enumerate((gg, gu)):
+        for h in range(2):
+            load_g.append(
+                local_copy(ref.at[:, pl.ds(h * half, half)], g_v.at[which, pl.ds(h * cfg.tok, cfg.tok)])
+            )
 
     load_act.wait()
     load_pp.wait()
@@ -150,18 +151,17 @@
     pl.semaphore_wait(barrier, len(partners))
 
     to_core = send(csend, crecv, core_peer)
-    moments = send(mm.at[zh], mm.at[zh], far_peer)
     load_pr.wait()
     rows_wide = dot_nt(pr_v[...], sel_v[...])
-    lane_quarter = lax.shift_right_logical(lax.broadcasted_iota(jnp.int32, rows_wide.shape, 1), 2) & 3
-    for q in range(4):
-        pw_v[q] = jnp.where(lane_quarter == q, rows_wide, 0.0).astype(BF16)
+    lane_half = lax.shift_right_logical(lax.broadcasted_iota(jnp.int32, rows_wide.shape, 1), 2) & 1
+    for h in range(2):
+        pw_v[h] = jnp.where(lane_half == h, rows_wide, 0.0).astype(BF16)
     save_pw = local_copy(pw_v, pw_out)
     to_core.wait_recv()
     mine = part_v[core] + crecv[...].astype(F32)
     zsend[...] = mine.astype(BF16)
     part_v[core] = mine
-    to_chips = [send(zsend, zrecv.at[d - 1], at_z(d)) for d in range(1, nzl)]
+    to_chips = [send(zsend, zrecv.at[d - 1], at_z(d)) for d in z_order]
     for copy in load_g:
         copy.wait()
     for copy in to_chips:
@@ -175,18 +175,18 @@
 
     basis = basis_v[...].reshape(cfg.tok, cfg.rank)
     basis_wide = dot_nt(sel_v[...], basis)
-    sub_quarter = lax.shift_right_logical(lax.broadcasted_iota(jnp.int32, basis_wide.shape, 0), 2) & 3
-    for q in range(4):
-        w_v[:, q * cfg.tok : (q + 1) * cfg.tok] = jnp.where(sub_quarter == q, basis_wide, 0.0).astype(BF16)
+    sub_half = lax.shift_right_logical(lax.broadcasted_iota(jnp.int32, basis_wide.shape, 0), 2) & 1
+    for h in range(2):
+        w_v[:, h * cfg.tok : (h + 1) * cfg.tok] = jnp.where(sub_half == h, basis_wide, 0.0).astype(BF16)
 
     def block(xblock, colour):
         return pl.ds(xblock * ny + colour * nyh, nyh)
 
     first = []
-    for k, (start, width) in enumerate(cfg.lanes):
+    for k, (which, start, width) in enumerate(cfg.chunks):
         p, rx1 = bufs["p"][k], bufs["rx1"][k]
-        grads = g_v[:, start : start + width]
-        p[...] = dot(w_v[...], grads).astype(BF16).reshape(cfg.pieces, 16, width)
+        grads = g_v[which, :, start : start + width]
+        p[...] = dot(w_v[...], grads).astype(BF16).reshape(cfg.pieces, 8, width)
         first.append(
             [
                 send(p.at[block(xa, 0)], rx1.at[0, 0], at_x(xa)),
@@ -196,14 +196,7 @@
             ]
         )
 
-    moments.wait_recv()
-    for which in range(2):
-        for end in range(2):
-            for j in range(2):
-                for q in range(4):
-                    ml[which, pl.ds(4 * q + 2 * end + j, 1), :] = mm[
-                        end, which, j, pl.ds(q // 2, 1), pl.ds((q % 2) * half, half)
-                    ]
+    moments = send(mm.at[zh], mm.at[zh], far_peer)
 
     second = []
     for k in range(nk):
@@ -224,7 +217,17 @@
         for colour in range(2):
             own = p[block(x, colour)].astype(F32) + rx1[colour, 0].astype(F32) + rx2[colour].astype(F32)
             sy[pl.ds(colour * nyh, nyh)] = own.astype(BF16)
-        third.append([send(sy.at[(y + d) % ny], ry.at[d - 1], at_y(d)) for d in range(1, ny)])
+        third.append([send(sy.at[(y + d) % ny], ry.at[d - 1], at_y(d)) for d in y_order])
+
+    moments.wait_recv()
+    for moment in range(2):
+        for end in range(2):
+            for j in range(2):
+                for which in range(2):
+                    for h in range(2):
+                        ml[moment, pl.ds(4 * h + 2 * end + j, 1), pl.ds(which * half, half)] = mm[
+                            end, moment, j, pl.ds(which, 1), pl.ds(h * half, half)
+                        ]
 
     fourth = []
     for k in range(nk):
@@ -241,16 +244,16 @@
     corr_one = 1.0 - 0.9**STEP
     corr_two = 1.0 - 0.999**STEP
     fifth = []
-    for k, (start, width) in enumerate(cfg.lanes):
+    for k, (which, start, width) in enumerate(cfg.chunks):
         rz, tf, g = (bufs[name][k] for name in ("rz", "tf", "g"))
         fourth[k].wait_recv()
-        cols = pl.ds(start, width)
+        cols = pl.ds(which * half + start, width)
         grad = tf[...] + rz[...].astype(F32)
         new_first = 0.9 * ml[0, :, cols] + 0.1 * grad
         new_second = 0.999 * ml[1, :, cols] + 0.001 * grad * grad
         step = new_first / corr_one / (jnp.sqrt(new_second / corr_two) + 1e-08)
         g[x * ny + y] = step.astype(BF16)
-        fifth.append([send(g.at[x * ny + y], g.at[x * ny + y], at_y(d)) for d in range(1, ny)])
+        fifth.append([send(g.at[x * ny + y], g.at[x * ny + y], at_y(d)) for d in y_order])
         nfl[:, cols] = new_first
         nsl[:, cols] = new_second
 
@@ -267,9 +270,12 @@
         sixth.append(copies)
 
     for j in range(2):
-        for q in range(4):
-            for flat, out in ((nfl, nf_out), (nsl, ns_out)):
-                out[j, pl.ds(q // 2, 1), pl.ds((q % 2) * half, half)] = flat[pl.ds(4 * q + j + 2 * zh, 1), :]
+        for which in range(2):
+            for h in range(2):
+                for flat, out in ((nfl, nf_out), (nsl, ns_out)):
+                    out[j, pl.ds(which, 1), pl.ds(h * half, half)] = flat[
+                        pl.ds(4 * h + j + 2 * zh, 1), pl.ds(which * half, half)
+                    ]
 
     seventh = []
     for k in range(nk):
@@ -307,13 +313,15 @@
     ns_out[...] = ns[...]
     loads[0].wait()
     saves = []
-    for k, (start, width) in enumerate(cfg.lanes):
+    for k, (which, start, width) in enumerate(cfg.chunks):
         loads[1 + k].wait()
-        steps = g_vs[k][...].reshape(cfg.pieces * 16, width)
-        for q, out in enumerate((gate, gate, up, up)):
-            out_vs[k][q] = dot(pw_v[q], steps).astype(BF16)
-            columns = pl.ds((q % 2) * cfg.half + start, width)
-            copy = pltpu.make_async_copy(out_vs[k].at[q], out.at[:, columns], sem.at[1 + nk + 4 * k + q])
+        steps = g_vs[k][...].reshape(cfg.pieces * 8, width)
+        for h in range(2):
+            out_vs[k][h] = dot(pw_v[h], steps).astype(BF16)
+            columns = pl.ds(h * cfg.half + start, width)
+            copy = pltpu.make_async_copy(
+                out_vs[k].at[h], (gate, up)[which].at[:, columns], sem.at[1 + nk + 2 * k + h]
+            )
             copy.start()
             saves.append(copy)
     for copy in saves:
@@ -323,55 +331,55 @@
 def shards(cfg, activations, projection, grad_gate, grad_up, first_moment, second_moment):
     nk = len(cfg.chunks)
     out_rows = projection.shape[0] // (2 * cfg.pieces)
-    wide, nyh, htok = cfg.pieces * 16, cfg.ny // 2, cfg.tok // 2
+    wide, nyh, htok = cfg.pieces * 8, cfg.ny // 2, cfg.tok // 2
     any_spec = pl.BlockSpec(memory_space=pl.ANY)
     vmem_spec = pl.BlockSpec(memory_space=pltpu.VMEM)
     small = jax.ShapeDtypeStruct(first_moment.shape, F32)
 
     def chunked(*shape, dtype=BF16):
-        return [pltpu.VMEM((*shape, width), dtype) for width in cfg.chunks]
+        return [pltpu.VMEM((*shape, width), dtype) for width in cfg.widths]
 
     remote_copies = 3 + (cfg.nzl - 1) + nk * (4 + 2 + 2 * (cfg.ny - 1) + 1 + 6)
     scratch = [
         pltpu.VMEM((cfg.tok, cfg.feat), BF16),
         pltpu.VMEM((cfg.feat, cfg.rank), BF16),
-        pltpu.VMEM((4 * cfg.tok, cfg.half), BF16),
+        pltpu.VMEM((2, 2 * cfg.tok, cfg.half), BF16),
         pltpu.VMEM((out_rows, cfg.rank), BF16),
         pltpu.VMEM((wide, cfg.rank), BF16),
-        pltpu.VMEM((4, out_rows, wide), BF16),
-        pltpu.VMEM((wide, 4 * cfg.tok), BF16),
+        pltpu.VMEM((2, out_rows, wide), BF16),
+        pltpu.VMEM((wide, 2 * cfg.tok), BF16),
         pltpu.VMEM((2, 2, 2, 2, cfg.ff), F32),
-        pltpu.VMEM((2, 16, cfg.half), F32),
-        pltpu.VMEM((16, cfg.half), F32),
-        pltpu.VMEM((16, cfg.half), F32),
+        pltpu.VMEM((2, 8, cfg.ff), F32),
+        pltpu.VMEM((8, cfg.ff), F32),
+        pltpu.VMEM((8, cfg.ff), F32),
         pltpu.VMEM((2, htok, cfg.rank), F32),
         pltpu.VMEM((htok, cfg.rank), BF16),
         pltpu.VMEM((htok, cfg.rank), BF16),
         pltpu.VMEM((htok, cfg.rank), BF16),
         pltpu.VMEM((cfg.nzl - 1, htok, cfg.rank), BF16),
         pltpu.VMEM((2, htok, cfg.rank), BF16),
-        *chunked(cfg.pieces, 16),
-        *chunked(2, 2, nyh, 16),
-        *chunked(2, nyh, 16),
-        *chunked(2, nyh, 16),
-        *chunked(cfg.ny, 16),
-        *chunked(cfg.ny - 1, 16),
-        *chunked(16),
-        *chunked(16),
-        *chunked(16, dtype=F32),
-        *chunked(cfg.pieces, 16),
+        *chunked(cfg.pieces, 8),
+        *chunked(2, 2, nyh, 8),
+        *chunked(2, nyh, 8),
+        *chunked(2, nyh, 8),
+        *chunked(cfg.ny, 8),
+        *chunked(cfg.ny - 1, 8),
+        *chunked(8),
+        *chunked(8),
+        *chunked(8, dtype=F32),
+        *chunked(cfg.pieces, 8),
         pltpu.SemaphoreType.DMA((10 + nk,)),
         pltpu.SemaphoreType.DMA((remote_copies,)),
         pltpu.SemaphoreType.DMA((remote_copies,)),
     ]
-    gathered = [jax.ShapeDtypeStruct((cfg.pieces, 16, width), BF16) for width in cfg.chunks]
+    gathered = [jax.ShapeDtypeStruct((cfg.pieces, 8, width), BF16) for width in cfg.widths]
     *steps, rows_wide, new_first, new_second = pl.pallas_call(
         functools.partial(comm_kernel, cfg),
-        out_shape=(*gathered, jax.ShapeDtypeStruct((4, out_rows, wide), BF16), small, small),
-        in_specs=[any_spec] * 6,
+        out_shape=(*gathered, jax.ShapeDtypeStruct((2, out_rows, wide), BF16), small, small),
+        in_specs=[pl.BlockSpec(memory_space=pltpu.HBM)] * 6,
         out_specs=(*[any_spec] * nk, any_spec, vmem_spec, vmem_spec),
         scratch_shapes=scratch,
-        compiler_params=pltpu.CompilerParams(collective_id=0, has_side_effects=True, vmem_limit_bytes=48 << 20),
+        compiler_params=pltpu.CompilerParams(collective_id=0, has_side_effects=True, vmem_limit_bytes=67043328),
         name="comm",
     )(activations, projection, grad_gate, grad_up, first_moment, second_moment)
     update = jax.ShapeDtypeStruct((out_rows, cfg.ff), BF16)
@@ -381,12 +389,12 @@
         in_specs=[any_spec] * (nk + 1) + [vmem_spec] * 2,
         out_specs=(any_spec, any_spec, vmem_spec, vmem_spec),
         scratch_shapes=[
-            *chunked(cfg.pieces, 16),
-            *chunked(4, out_rows),
-            pltpu.VMEM((4, out_rows, wide), BF16),
-            pltpu.SemaphoreType.DMA((1 + 5 * nk,)),
+            *chunked(cfg.pieces, 8),
+            *chunked(2, out_rows),
+            pltpu.VMEM((2, out_rows, wide), BF16),
+            pltpu.SemaphoreType.DMA((1 + 3 * nk,)),
         ],
-        compiler_params=pltpu.CompilerParams(vmem_limit_bytes=48 << 20),
+        compiler_params=pltpu.CompilerParams(vmem_limit_bytes=67043328),
         name="update",
     )(*steps, rows_wide, new_first, new_second)
 
@@ -412,4 +420,4 @@
 
 
 def solution(mesh):
-    return build(mesh, Cfg(ny=8, nzl=8, tok=128, feat=512, ff=1792, chunks=(512, 384)))
+    return build(mesh, Cfg(ny=8, nzl=8, tok=128, feat=512, ff=1792, chunks=((0, 0, 896), (1, 0, 896))))

time: 84.9 us -> 76.6 us (0.902)
  the two profiles are of different devices: /device:TPU:64 before, /device:TPU:2 now
where the time goes in v2:
time: 76.6 us; the launch traced here: 76.4 us
  Pallas kernels  75.7 us (99%)
    pallas_call x1, Pallas kernels, shards(): pl.pallas_call(functools.partial(comm_kernel, cfg), out_shape=(*gathered,...  71.9 us
    pallas_call x1, Pallas kernels, shards(): pl.pallas_call(functools.partial(update_kernel, cfg), out_shape=(update,...  3.85 us

profile of v2, /device:TPU:2, one launch (start us, length us, event | category | flops | bytes accessed | tf_op | source)
XLA Modules:
  0.0 76.4 jit_solution(12894787488387668967)
XLA Ops:
  0.6 71.9 %comm.1 = (bf16[32,8,896]{2,1,0:T(8,128)(2,1)}, bf16[32,8,896]{2,1,0:T(8,128)(2,1)}, bf16[2,128,256]{2,1,0:T(8,128)(2,1)}, f32[2,2,1792]{2,1,0:T(2,128)}, f32[2,2,1792]{2,1,0:T(2,128)}) custom-call(bf16[128,512]{1,0:T(8,128)(2,1)} %refs_0_.1, bf16[8192,128]{1,0:T(8,128)(2,1)} %refs_1_.1, bf16[128,1792]{1,0:T(8,128)(2,1)} %refs_2_.1, ...), custom_call_target="tpu_custom_call" | custom-call | tf_op jit(solution)/shard_map/comm/pallas_call | solution.py:376
  72.5 3.9 %update.1 = (bf16[128,1792]{1,0:T(8,128)(2,1)}, bf16[128,1792]{1,0:T(8,128)(2,1)}, f32[2,2,1792]{2,1,0:T(2,128)}, f32[2,2,1792]{2,1,0:T(2,128)}) custom-call(bf16[32,8,896]{2,1,0:T(8,128)(2,1)} %get-tuple-element.9.refs_0_, bf16[32,8,896]{2,1,0:T(8,128)(2,1)} %get-tuple-element.10.refs_1_, bf16[2,128,256]{2,1,0:T(8,128)(2,1)} %get-tuple-element.11.refs_2_, ...), custom_call_target="tpu_custom_call" | custom-call | tf_op jit(solution)/shard_map/update/pallas_call | solution.py:386

commit v3 on v2

--- a/solution.py
+++ b/solution.py
@@ -65,14 +65,14 @@
 def comm_kernel(cfg, *refs):
     nk = len(cfg.chunks)
     nx, ny, nzl, half = cfg.nx, cfg.ny, cfg.nzl, cfg.half
-    nyh, htok = ny // 2, cfg.tok // 2
+    nyh, zhalf, htok = ny // 2, nzl // 2, cfg.tok // 2
     (act, proj, gg, gu, m1, m2), refs = refs[:6], refs[6:]
     g_outs, refs = refs[:nk], refs[nk:]
     (pw_out, nf_out, ns_out), refs = refs[:3], refs[3:]
     (act_v, pp_v, g_v, pr_v, sel_v, pw_v, w_v, mm, ml, nfl, nsl), refs = refs[:11], refs[11:]
-    (part_v, csend, crecv, zsend, zrecv, basis_v), refs = refs[:6], refs[6:]
-    names = ("p", "rx1", "sx2", "rx2", "sy", "ry", "sz", "rz", "tf", "g")
-    bufs = {}
+    (part_v, csend, crecv, zsend, zpair, zrecv, basis_v), refs = refs[:7], refs[7:]
+    names = ("p", "rx1", "sx2", "rx2", "sy", "ry", "sz", "rz", "tf")
+    bufs = {"g": g_outs}
     for name in names:
         bufs[name], refs = refs[:nk], refs[nk:]
     load_sem, send_sem, recv_sem = refs
@@ -94,11 +94,13 @@
         return (dp, ((zl + d) % nzl) * 2 + core)
 
     y_order = sorted(range(1, ny), key=lambda d: -min(d, ny - d))
-    z_order = list(range(nzl - 1, 0, -1))
+    def at_z_half(d):
+        return (dp, ((zl // zhalf) * zhalf + (zl + d) % zhalf) * 2 + core)
+
     core_peer = (dp, zl * 2 + 1 - core)
     far_peer = ((x * 2 + 1 - zh) * ny + y, tensor)
     partners = [core_peer, far_peer, at_x(xa), at_x(xb)]
-    partners += [at_z(d) for d in range(1, nzl)] + [at_y(d) for d in range(1, ny)]
+    partners += [at_z(zhalf)] + [at_z_half(d) for d in range(1, zhalf)] + [at_y(d) for d in range(1, ny)]
 
     counts = {"local": 0, "remote": 0}
     remote = []
@@ -161,14 +163,19 @@
     mine = part_v[core] + crecv[...].astype(F32)
     zsend[...] = mine.astype(BF16)
     part_v[core] = mine
-    to_chips = [send(zsend, zrecv.at[d - 1], at_z(d)) for d in z_order]
+    across = send(zsend, zrecv.at[0], at_z(zhalf))
     for copy in load_g:
         copy.wait()
+    across.wait_recv()
+    pair = part_v[core] + zrecv[0].astype(F32)
+    zpair[...] = pair.astype(BF16)
+    part_v[core] = pair
+    to_chips = [send(zpair, zrecv.at[d], at_z_half(d)) for d in range(zhalf - 1, 0, -1)]
     for copy in to_chips:
         copy.wait_recv()
     total = part_v[core]
-    for d in range(1, nzl):
-        total = total + zrecv[d - 1].astype(F32)
+    for d in range(1, zhalf):
+        total = total + zrecv[d].astype(F32)
     basis_v[core] = total.astype(BF16)
     finished = send(basis_v.at[core], basis_v.at[core], core_peer)
     finished.wait_recv()
@@ -286,49 +293,38 @@
             copies.append(send(g.at[block(near, colour)], g.at[block(near, colour)], at_x(far)))
         seventh.append(copies)
 
-    saves = []
     for k in range(nk):
         for copy in sixth[k][2:] + seventh[k]:
             copy.wait_recv()
-        saves.append(local_copy(bufs["g"][k], g_outs[k]))
     for copy in remote:
         copy.wait_send()
     save_pw.wait()
-    for copy in saves:
-        copy.wait()
 
 
 def update_kernel(cfg, *refs):
     nk = len(cfg.chunks)
     gs, refs = refs[:nk], refs[nk:]
     pw, nf, ns, gate, up, nf_out, ns_out, refs = *refs[:7], refs[7:]
-    g_vs, refs = refs[:nk], refs[nk:]
-    out_vs, refs = refs[:nk], refs[nk:]
-    pw_v, sem = refs
-    loads = [pltpu.make_async_copy(pw, pw_v, sem.at[0])]
-    loads += [pltpu.make_async_copy(gs[k], g_vs[k], sem.at[1 + k]) for k in range(nk)]
-    for copy in loads:
-        copy.start()
-    nf_out[...] = nf[...]
-    ns_out[...] = ns[...]
-    loads[0].wait()
+    out_vs, (sem,) = refs[:nk], refs[nk:]
     saves = []
     for k, (which, start, width) in enumerate(cfg.chunks):
-        loads[1 + k].wait()
-        steps = g_vs[k][...].reshape(cfg.pieces * 8, width)
+        steps = gs[k][...].reshape(cfg.pieces * 8, width)
         for h in range(2):
-            out_vs[k][h] = dot(pw_v[h], steps).astype(BF16)
+            out_vs[k][h] = dot(pw[h], steps).astype(BF16)
             columns = pl.ds(h * cfg.half + start, width)
             copy = pltpu.make_async_copy(
-                out_vs[k].at[h], (gate, up)[which].at[:, columns], sem.at[1 + nk + 2 * k + h]
+                out_vs[k].at[h], (gate, up)[which].at[:, columns], sem.at[2 * k + h]
             )
             copy.start()
             saves.append(copy)
+    nf_out[...] = nf[...]
+    ns_out[...] = ns[...]
     for copy in saves:
         copy.wait()
 
 
-def shards(cfg, activations, projection, grad_gate, grad_up, first_moment, second_moment):
+def shards(cfg, *inputs):
+    _, projection, _, _, first_moment, _ = inputs
     nk = len(cfg.chunks)
     out_rows = projection.shape[0] // (2 * cfg.pieces)
     wide, nyh, htok = cfg.pieces * 8, cfg.ny // 2, cfg.tok // 2
@@ -339,7 +335,7 @@
     def chunked(*shape, dtype=BF16):
         return [pltpu.VMEM((*shape, width), dtype) for width in cfg.widths]
 
-    remote_copies = 3 + (cfg.nzl - 1) + nk * (4 + 2 + 2 * (cfg.ny - 1) + 1 + 6)
+    remote_copies = 3 + cfg.nzl // 2 + nk * (4 + 2 + 2 * (cfg.ny - 1) + 1 + 6)
     scratch = [
         pltpu.VMEM((cfg.tok, cfg.feat), BF16),
         pltpu.VMEM((cfg.feat, cfg.rank), BF16),
@@ -356,7 +352,8 @@
         pltpu.VMEM((htok, cfg.rank), BF16),
         pltpu.VMEM((htok, cfg.rank), BF16),
         pltpu.VMEM((htok, cfg.rank), BF16),
-        pltpu.VMEM((cfg.nzl - 1, htok, cfg.rank), BF16),
+        pltpu.VMEM((htok, cfg.rank), BF16),
+        pltpu.VMEM((cfg.nzl // 2, htok, cfg.rank), BF16),
         pltpu.VMEM((2, htok, cfg.rank), BF16),
         *chunked(cfg.pieces, 8),
         *chunked(2, 2, nyh, 8),
@@ -367,34 +364,31 @@
         *chunked(8),
         *chunked(8),
         *chunked(8, dtype=F32),
-        *chunked(cfg.pieces, 8),
-        pltpu.SemaphoreType.DMA((10 + nk,)),
+        pltpu.SemaphoreType.DMA((10,)),
         pltpu.SemaphoreType.DMA((remote_copies,)),
         pltpu.SemaphoreType.DMA((remote_copies,)),
     ]
-    gathered = [jax.ShapeDtypeStruct((cfg.pieces, 8, width), BF16) for width in cfg.widths]
+    gathered = chunked(cfg.pieces, 8)
     *steps, rows_wide, new_first, new_second = pl.pallas_call(
         functools.partial(comm_kernel, cfg),
         out_shape=(*gathered, jax.ShapeDtypeStruct((2, out_rows, wide), BF16), small, small),
         in_specs=[pl.BlockSpec(memory_space=pltpu.HBM)] * 6,
-        out_specs=(*[any_spec] * nk, any_spec, vmem_spec, vmem_spec),
+        out_specs=(*[vmem_spec] * nk, any_spec, vmem_spec, vmem_spec),
         scratch_shapes=scratch,
-        compiler_params=pltpu.CompilerParams(collective_id=0, has_side_effects=True, vmem_limit_bytes=67043328),
+        compiler_params=pltpu.CompilerParams(collective_id=0, has_side_effects=True, vmem_limit_bytes=48 << 20),
         name="comm",
-    )(activations, projection, grad_gate, grad_up, first_moment, second_moment)
+    )(*[pltpu.with_memory_space_constraint(ref, pltpu.HBM) for ref in inputs])
     update = jax.ShapeDtypeStruct((out_rows, cfg.ff), BF16)
     return pl.pallas_call(
         functools.partial(update_kernel, cfg),
         out_shape=(update, update, small, small),
-        in_specs=[any_spec] * (nk + 1) + [vmem_spec] * 2,
+        in_specs=[vmem_spec] * (nk + 3),
         out_specs=(any_spec, any_spec, vmem_spec, vmem_spec),
         scratch_shapes=[
-            *chunked(cfg.pieces, 8),
             *chunked(2, out_rows),
-            pltpu.VMEM((2, out_rows, wide), BF16),
-            pltpu.SemaphoreType.DMA((1 + 3 * nk,)),
+            pltpu.SemaphoreType.DMA((2 * nk,)),
         ],
-        compiler_params=pltpu.CompilerParams(vmem_limit_bytes=67043328),
+        compiler_params=pltpu.CompilerParams(vmem_limit_bytes=48 << 20),
         name="update",
     )(*steps, rows_wide, new_first, new_second)
 
@@ -420,4 +414,4 @@
 
 
 def solution(mesh):
-    return build(mesh, Cfg(ny=8, nzl=8, tok=128, feat=512, ff=1792, chunks=((0, 0, 896), (1, 0, 896))))
+    return build(mesh, Cfg(ny=8, nzl=8, tok=128, feat=512, ff=1792, chunks=((0, 0, 512), (0, 512, 384), (1, 0, 512), (1, 512, 384))))

time: 76.6 us -> 71.8 us (0.937)
  the two profiles are of different devices: /device:TPU:2 before, /device:TPU:1 now
where the time goes in v3:
time: 71.8 us; the launch traced here: 71.2 us
  Pallas kernels  70.6 us (98%)
    pallas_call x1, Pallas kernels, shards(): pl.pallas_call(functools.partial(comm_kernel, cfg), out_shape=(*gathered,...  68.8 us
    pallas_call x1, Pallas kernels, shards(): pl.pallas_call(functools.partial(update_kernel, cfg), out_shape=(update,...  1.8 us

profile of v3, /device:TPU:1, one launch (start us, length us, event | category | flops | bytes accessed | tf_op | source)
XLA Modules:
  0.0 71.2 jit_solution(15067717654804961880)
XLA Ops:
  0.6 68.8 %comm.1 = (bf16[32,8,512]{2,1,0:T(8,128)(2,1)S(1)}, bf16[32,8,384]{2,1,0:T(8,128)(2,1)S(1)}, bf16[32,8,512]{2,1,0:T(8,128)(2,1)S(1)}, bf16[32,8,384]{2,1,0:T(8,1...) custom-call(bf16[128,512]{1,0:T(8,128)(2,1)} %refs_0_.1, ...), custom_call_target="tpu_custom_call" | custom-call | tf_op jit(solution)/shard_map/comm/pallas_call | solution.py:372
  69.4 1.8 %update.1 = (bf16[128,1792]{1,0:T(8,128)(2,1)}, bf16[128,1792]{1,0:T(8,128)(2,1)}, f32[2,2,1792]{2,1,0:T(2,128)}, f32[2,2,1792]{2,1,0:T(2,128)}) custom-call(bf16[32,8,512]{2,1,0:T(8,128)(2,1)S(1)} %get-tuple-element.11.refs_0_, bf16[32,8,384]{2,1,0:T(8,128)(2,1)S(1)} %get-tuple-element.12.refs_1_, bf16[32,8,512]{2,1,0:T(8,128)(2,1)S(1)} %get-tuple-element.13.refs_2_, ...), custom_call_target="tpu_custom_call" | custom-call | tf_op jit(solution)/shard_map/update/pallas_call | solution.py:382

commit v4 on v3

--- a/solution.py
+++ b/solution.py
@@ -65,13 +65,13 @@
 def comm_kernel(cfg, *refs):
     nk = len(cfg.chunks)
     nx, ny, nzl, half = cfg.nx, cfg.ny, cfg.nzl, cfg.half
-    nyh, zhalf, htok = ny // 2, nzl // 2, cfg.tok // 2
+    zhalf, htok = nzl // 2, cfg.tok // 2
     (act, proj, gg, gu, m1, m2), refs = refs[:6], refs[6:]
     g_outs, refs = refs[:nk], refs[nk:]
     (pw_out, nf_out, ns_out), refs = refs[:3], refs[3:]
     (act_v, pp_v, g_v, pr_v, sel_v, pw_v, w_v, mm, ml, nfl, nsl), refs = refs[:11], refs[11:]
     (part_v, csend, crecv, zsend, zpair, zrecv, basis_v), refs = refs[:7], refs[7:]
-    names = ("p", "rx1", "sx2", "rx2", "sy", "ry", "sz", "rz", "tf")
+    names = ("p", "rx", "sy", "ry", "sz", "rz", "tf")
     bufs = {"g": g_outs}
     for name in names:
         bufs[name], refs = refs[:nk], refs[nk:]
@@ -80,9 +80,6 @@
     dp, tensor = lax.axis_index("dp"), lax.axis_index("tensor")
     core, zl = tensor % 2, tensor // 2
     y, zh, x = dp % ny, (dp // ny) % 2, dp // (2 * ny)
-    xa = x + 1 - 2 * (x % 2)
-    xb = (nx - 1) - x
-    xo = (x + 2) % nx
 
     def at_x(other):
         return ((other * 2 + zh) * ny + y, tensor)
@@ -94,12 +91,13 @@
         return (dp, ((zl + d) % nzl) * 2 + core)
 
     y_order = sorted(range(1, ny), key=lambda d: -min(d, ny - d))
+    x_order = sorted(range(1, nx), key=lambda d: -min(d, nx - d))
     def at_z_half(d):
         return (dp, ((zl // zhalf) * zhalf + (zl + d) % zhalf) * 2 + core)
 
     core_peer = (dp, zl * 2 + 1 - core)
     far_peer = ((x * 2 + 1 - zh) * ny + y, tensor)
-    partners = [core_peer, far_peer, at_x(xa), at_x(xb)]
+    partners = [core_peer, far_peer, *[at_x((x + d) % nx) for d in range(1, nx)]]
     partners += [at_z(zhalf)] + [at_z_half(d) for d in range(1, zhalf)] + [at_y(d) for d in range(1, ny)]
 
     counts = {"local": 0, "remote": 0}
@@ -186,44 +184,27 @@
     for h in range(2):
         w_v[:, h * cfg.tok : (h + 1) * cfg.tok] = jnp.where(sub_half == h, basis_wide, 0.0).astype(BF16)
 
-    def block(xblock, colour):
-        return pl.ds(xblock * ny + colour * nyh, nyh)
+    def block(xblock):
+        return pl.ds(xblock * ny, ny)
 
     first = []
     for k, (which, start, width) in enumerate(cfg.chunks):
-        p, rx1 = bufs["p"][k], bufs["rx1"][k]
+        p, rx = bufs["p"][k], bufs["rx"][k]
         grads = g_v[which, :, start : start + width]
         p[...] = dot(w_v[...], grads).astype(BF16).reshape(cfg.pieces, 8, width)
-        first.append(
-            [
-                send(p.at[block(xa, 0)], rx1.at[0, 0], at_x(xa)),
-                send(p.at[block(xb, 1)], rx1.at[1, 0], at_x(xb)),
-                send(p.at[block(xo, 0)], rx1.at[0, 1], at_x(xa)),
-                send(p.at[block(xo, 1)], rx1.at[1, 1], at_x(xb)),
-            ]
-        )
+        first.append([send(p.at[block((x + d) % nx)], rx.at[d - 1], at_x((x + d) % nx)) for d in x_order])
 
     moments = send(mm.at[zh], mm.at[zh], far_peer)
 
-    second = []
+    third = []
     for k in range(nk):
-        p, rx1, sx2, rx2 = (bufs[name][k] for name in ("p", "rx1", "sx2", "rx2"))
+        p, rx, sy, ry = (bufs[name][k] for name in ("p", "rx", "sy", "ry"))
         for copy in first[k]:
             copy.wait_recv()
-        copies = []
-        for colour, other in ((0, xb), (1, xa)):
-            sx2[colour] = (p[block(other, colour)].astype(F32) + rx1[colour, 1].astype(F32)).astype(BF16)
-            copies.append(send(sx2.at[colour], rx2.at[colour], at_x(other)))
-        second.append(copies)
-
-    third = []
-    for k in range(nk):
-        p, rx1, rx2, sy, ry = (bufs[name][k] for name in ("p", "rx1", "rx2", "sy", "ry"))
-        for copy in second[k]:
-            copy.wait_recv()
-        for colour in range(2):
-            own = p[block(x, colour)].astype(F32) + rx1[colour, 0].astype(F32) + rx2[colour].astype(F32)
-            sy[pl.ds(colour * nyh, nyh)] = own.astype(BF16)
+        own = p[block(x)].astype(F32)
+        for d in range(1, nx):
+            own = own + rx[d - 1].astype(F32)
+        sy[...] = own.astype(BF16)
         third.append([send(sy.at[(y + d) % ny], ry.at[d - 1], at_y(d)) for d in y_order])
 
     moments.wait_recv()
@@ -269,12 +250,8 @@
         g = bufs["g"][k]
         for copy in fifth[k]:
             copy.wait_recv()
-        copies = []
-        for colour, near, far in ((0, xb, xa), (1, xa, xb)):
-            copies.append(send(g.at[block(x, colour)], g.at[block(x, colour)], at_x(near)))
-        for colour, near, far in ((0, xb, xa), (1, xa, xb)):
-            copies.append(send(g.at[block(x, colour)], g.at[block(x, colour)], at_x(far)))
-        sixth.append(copies)
+        own = block(x)
+        sixth.append([send(g.at[own], g.at[own], at_x((x + d) % nx)) for d in x_order])
 
     for j in range(2):
         for which in range(2):
@@ -284,17 +261,8 @@
                         pl.ds(4 * h + j + 2 * zh, 1), pl.ds(which * half, half)
                     ]
 
-    seventh = []
     for k in range(nk):
-        g = bufs["g"][k]
-        copies = []
-        for colour, near, far in ((0, xb, xa), (1, xa, xb)):
-            sixth[k][colour].wait_recv()
-            copies.append(send(g.at[block(near, colour)], g.at[block(near, colour)], at_x(far)))
-        seventh.append(copies)
-
-    for k in range(nk):
-        for copy in sixth[k][2:] + seventh[k]:
+        for copy in sixth[k]:
             copy.wait_recv()
     for copy in remote:
         copy.wait_send()
@@ -327,7 +295,7 @@
     _, projection, _, _, first_moment, _ = inputs
     nk = len(cfg.chunks)
     out_rows = projection.shape[0] // (2 * cfg.pieces)
-    wide, nyh, htok = cfg.pieces * 8, cfg.ny // 2, cfg.tok // 2
+    wide, htok = cfg.pieces * 8, cfg.tok // 2
     any_spec = pl.BlockSpec(memory_space=pl.ANY)
     vmem_spec = pl.BlockSpec(memory_space=pltpu.VMEM)
     small = jax.ShapeDtypeStruct(first_moment.shape, F32)
@@ -335,7 +303,7 @@
     def chunked(*shape, dtype=BF16):
         return [pltpu.VMEM((*shape, width), dtype) for width in cfg.widths]
 
-    remote_copies = 3 + cfg.nzl // 2 + nk * (4 + 2 + 2 * (cfg.ny - 1) + 1 + 6)
+    remote_copies = 3 + cfg.nzl // 2 + nk * (2 * (cfg.nx - 1) + 2 * (cfg.ny - 1) + 1)
     scratch = [
         pltpu.VMEM((cfg.tok, cfg.feat), BF16),
         pltpu.VMEM((cfg.feat, cfg.rank), BF16),
@@ -356,9 +324,7 @@
         pltpu.VMEM((cfg.nzl // 2, htok, cfg.rank), BF16),
         pltpu.VMEM((2, htok, cfg.rank), BF16),
         *chunked(cfg.pieces, 8),
-        *chunked(2, 2, nyh, 8),
-        *chunked(2, nyh, 8),
-        *chunked(2, nyh, 8),
+        *chunked(cfg.nx - 1, cfg.ny, 8),
         *chunked(cfg.ny, 8),
         *chunked(cfg.ny - 1, 8),
         *chunked(8),
@@ -414,4 +380,4 @@
 
 
 def solution(mesh):
-    return build(mesh, Cfg(ny=8, nzl=8, tok=128, feat=512, ff=1792, chunks=((0, 0, 512), (0, 512, 384), (1, 0, 512), (1, 512, 384))))
+    return build(mesh, Cfg(ny=8, nzl=8, tok=128, feat=512, ff=1792, chunks=((0, 0, 384), (0, 384, 512), (1, 0, 512), (1, 512, 256), (1, 768, 128))))

time: 71.8 us -> 71.3 us (level)
  no operation moved by 1% of the time
where the time goes in v4:
time: 71.3 us; the launch traced here: 71.2 us
  Pallas kernels  70.5 us (99%)
    pallas_call x1, Pallas kernels, shards(): pl.pallas_call(functools.partial(comm_kernel, cfg), out_shape=(*gathered,...  68.7 us
    pallas_call x1, Pallas kernels, shards(): pl.pallas_call(functools.partial(update_kernel, cfg), out_shape=(update,...  1.82 us

profile of v4, /device:TPU:1, one launch (start us, length us, event | category | flops | bytes accessed | tf_op | source)
XLA Modules:
  0.0 71.2 jit_solution(16481418141970097737)
XLA Ops:
  0.6 68.7 %comm.1 = (bf16[32,8,384]{2,1,0:T(8,128)(2,1)S(1)}, bf16[32,8,512]{2,1,0:T(8,128)(2,1)S(1)}, bf16[32,8,512]{2,1,0:T(8,128)(2,1)S(1)}, bf16[32,8,256]{2,1,0:T(8,1...) custom-call(bf16[128,512]{1,0:T(8,128)(2,1)} %refs_0_.1, ...), custom_call_target="tpu_custom_call" | custom-call | tf_op jit(solution)/shard_map/comm/pallas_call | solution.py:338
  69.4 1.8 %update.1 = (bf16[128,1792]{1,0:T(8,128)(2,1)}, bf16[128,1792]{1,0:T(8,128)(2,1)}, f32[2,2,1792]{2,1,0:T(2,128)}, f32[2,2,1792]{2,1,0:T(2,128)}) custom-call(bf16[32,8,384]{2,1,0:T(8,128)(2,1)S(1)} %get-tuple-element.12.refs_0_, bf16[32,8,512]{2,1,0:T(8,128)(2,1)S(1)} %get-tuple-element.13.refs_1_, bf16[32,8,512]{2,1,0:T(8,128)(2,1)S(1)} %get-tuple-element.14.refs_2_, ...), custom_call_target="tpu_custom_call" | custom-call | tf_op jit(solution)/shard_map/update/pallas_call | solution.py:348

commit v5 on v4

--- a/solution.py
+++ b/solution.py
@@ -70,7 +70,7 @@
     g_outs, refs = refs[:nk], refs[nk:]
     (pw_out, nf_out, ns_out), refs = refs[:3], refs[3:]
     (act_v, pp_v, g_v, pr_v, sel_v, pw_v, w_v, mm, ml, nfl, nsl), refs = refs[:11], refs[11:]
-    (part_v, csend, crecv, zsend, zpair, zrecv, basis_v), refs = refs[:7], refs[7:]
+    (part_v, psend, precv, zpair, zrecv, basis_v), refs = refs[:6], refs[6:]
     names = ("p", "rx", "sy", "ry", "sz", "rz", "tf")
     bufs = {"g": g_outs}
     for name in names:
@@ -87,18 +87,21 @@
     def at_y(d):
         return ((x * 2 + zh) * ny + (y + d) % ny, tensor)
 
-    def at_z(d):
-        return (dp, ((zl + d) % nzl) * 2 + core)
+    def at_z(d, other):
+        return (dp, ((zl + d) % nzl) * 2 + other)
 
     y_order = sorted(range(1, ny), key=lambda d: -min(d, ny - d))
     x_order = sorted(range(1, nx), key=lambda d: -min(d, nx - d))
-    def at_z_half(d):
-        return (dp, ((zl // zhalf) * zhalf + (zl + d) % zhalf) * 2 + core)
+    def at_z_half(d, other):
+        return (dp, ((zl // zhalf) * zhalf + (zl + d) % zhalf) * 2 + other)
 
     core_peer = (dp, zl * 2 + 1 - core)
     far_peer = ((x * 2 + 1 - zh) * ny + y, tensor)
     partners = [core_peer, far_peer, *[at_x((x + d) % nx) for d in range(1, nx)]]
-    partners += [at_z(zhalf)] + [at_z_half(d) for d in range(1, zhalf)] + [at_y(d) for d in range(1, ny)]
+    cores = (core, 1 - core)
+    partners += [at_z(zhalf, other) for other in cores]
+    partners += [at_z_half(d, other) for d in range(1, zhalf) for other in cores]
+    partners += [at_y(d) for d in range(1, ny)]
 
     counts = {"local": 0, "remote": 0}
     remote = []
@@ -143,40 +146,46 @@
     load_pp.wait()
     part = dot(act_v[...], pp_v[...])
     part_v[...] = part.reshape(2, htok, cfg.rank)
-    csend[...] = part_v[1 - core].astype(BF16)
+    psend[...] = part_v[...].astype(BF16)
     sel_v[...] = row_select(cfg)
     for copy in load_m:
         copy.wait()
 
     pl.semaphore_wait(barrier, len(partners))
 
-    to_core = send(csend, crecv, core_peer)
+    near = [
+        send(psend.at[core], precv.at[0], at_z(zhalf, core)),
+        send(psend.at[1 - core], precv.at[1], at_z(zhalf, 1 - core)),
+        send(psend.at[1 - core], precv.at[2], core_peer),
+    ]
     load_pr.wait()
     rows_wide = dot_nt(pr_v[...], sel_v[...])
     lane_half = lax.shift_right_logical(lax.broadcasted_iota(jnp.int32, rows_wide.shape, 1), 2) & 1
     for h in range(2):
         pw_v[h] = jnp.where(lane_half == h, rows_wide, 0.0).astype(BF16)
     save_pw = local_copy(pw_v, pw_out)
-    to_core.wait_recv()
-    mine = part_v[core] + crecv[...].astype(F32)
-    zsend[...] = mine.astype(BF16)
-    part_v[core] = mine
-    across = send(zsend, zrecv.at[0], at_z(zhalf))
+    for copy in near:
+        copy.wait_recv()
+    pair = part_v[core] + (precv[0].astype(F32) + precv[1].astype(F32) + precv[2].astype(F32))
+    zpair[...] = pair.astype(BF16)
+    part_v[core] = pair
+    to_chips = []
+    for d in range(zhalf - 1, 0, -1):
+        for mine, other in enumerate(cores):
+            to_chips.append(send(zpair, zrecv.at[mine, d], at_z_half(d, other)))
+    to_chips.append(send(zpair, zrecv.at[1, 0], core_peer))
     for copy in load_g:
         copy.wait()
-    across.wait_recv()
-    pair = part_v[core] + zrecv[0].astype(F32)
-    zpair[...] = pair.astype(BF16)
-    part_v[core] = pair
-    to_chips = [send(zpair, zrecv.at[d], at_z_half(d)) for d in range(zhalf - 1, 0, -1)]
     for copy in to_chips:
         copy.wait_recv()
     total = part_v[core]
     for d in range(1, zhalf):
-        total = total + zrecv[d].astype(F32)
+        total = total + zrecv[0, d].astype(F32)
     basis_v[core] = total.astype(BF16)
-    finished = send(basis_v.at[core], basis_v.at[core], core_peer)
-    finished.wait_recv()
+    total = zrecv[1, 0].astype(F32)
+    for d in range(1, zhalf):
+        total = total + zrecv[1, d].astype(F32)
+    basis_v[1 - core] = total.astype(BF16)
 
     basis = basis_v[...].reshape(cfg.tok, cfg.rank)
     basis_wide = dot_nt(sel_v[...], basis)
@@ -303,7 +312,7 @@
     def chunked(*shape, dtype=BF16):
         return [pltpu.VMEM((*shape, width), dtype) for width in cfg.widths]
 
-    remote_copies = 3 + cfg.nzl // 2 + nk * (2 * (cfg.nx - 1) + 2 * (cfg.ny - 1) + 1)
+    remote_copies = 3 + cfg.nzl + nk * (2 * (cfg.nx - 1) + 2 * (cfg.ny - 1) + 1)
     scratch = [
         pltpu.VMEM((cfg.tok, cfg.feat), BF16),
         pltpu.VMEM((cfg.feat, cfg.rank), BF16),
@@ -317,11 +326,10 @@
         pltpu.VMEM((8, cfg.ff), F32),
         pltpu.VMEM((8, cfg.ff), F32),
         pltpu.VMEM((2, htok, cfg.rank), F32),
+        pltpu.VMEM((2, htok, cfg.rank), BF16),
+        pltpu.VMEM((3, htok, cfg.rank), BF16),
         pltpu.VMEM((htok, cfg.rank), BF16),
-        pltpu.VMEM((htok, cfg.rank), BF16),
-        pltpu.VMEM((htok, cfg.rank), BF16),
-        pltpu.VMEM((htok, cfg.rank), BF16),
-        pltpu.VMEM((cfg.nzl // 2, htok, cfg.rank), BF16),
+        pltpu.VMEM((2, cfg.nzl // 2, htok, cfg.rank), BF16),
         pltpu.VMEM((2, htok, cfg.rank), BF16),
         *chunked(cfg.pieces, 8),
         *chunked(cfg.nx - 1, cfg.ny, 8),

time: 71.3 us -> 70.8 us (level); the launches traced: 71.2 us -> 69.7 us
  Pallas kernels: 70.5 us -> 69.1 us
    pallas_call x1, Pallas kernels: 68.7 us -> 67.2 us  [shards(): pl.pallas_call(functools.partial(comm_kernel, cfg), out_shape=(*gathered,...]
where the time goes in v5:
time: 70.8 us; the launch traced here: 69.7 us
  Pallas kernels  69.1 us (98%)
    pallas_call x1, Pallas kernels, shards(): pl.pallas_call(functools.partial(comm_kernel, cfg), out_shape=(*gathered,...  67.2 us
    pallas_call x1, Pallas kernels, shards(): pl.pallas_call(functools.partial(update_kernel, cfg), out_shape=(update,...  1.81 us

profile of v5, /device:TPU:1, one launch (start us, length us, event | category | flops | bytes accessed | tf_op | source)
XLA Modules:
  0.0 69.7 jit_solution(18268359139161366094)
XLA Ops:
  0.6 67.2 %comm.1 = (bf16[32,8,384]{2,1,0:T(8,128)(2,1)S(1)}, bf16[32,8,512]{2,1,0:T(8,128)(2,1)S(1)}, bf16[32,8,512]{2,1,0:T(8,128)(2,1)S(1)}, bf16[32,8,256]{2,1,0:T(8,1...) custom-call(bf16[128,512]{1,0:T(8,128)(2,1)} %refs_0_.1, ...), custom_call_target="tpu_custom_call" | custom-call | tf_op jit(solution)/shard_map/comm/pallas_call | solution.py:346
  67.9 1.8 %update.1 = (bf16[128,1792]{1,0:T(8,128)(2,1)}, bf16[128,1792]{1,0:T(8,128)(2,1)}, f32[2,2,1792]{2,1,0:T(2,128)}, f32[2,2,1792]{2,1,0:T(2,128)}) custom-call(bf16[32,8,384]{2,1,0:T(8,128)(2,1)S(1)} %get-tuple-element.12.refs_0_, bf16[32,8,512]{2,1,0:T(8,128)(2,1)S(1)} %get-tuple-element.13.refs_1_, bf16[32,8,512]{2,1,0:T(8,128)(2,1)S(1)} %get-tuple-element.14.refs_2_, ...), custom_call_target="tpu_custom_call" | custom-call | tf_op jit(solution)/shard_map/update/pallas_call | solution.py:356
